TPU v7x, 32 devices: a whole 2x2x4 slice. The times are simulated.
32 devices in a mesh: groups: 2 (over y), space: 8 (over z, x), dp: 2 (over core).
Axes of the slice: x: 2, y: 2, z: 4, core: 2. Of those that a mesh axis runs over, the one named last changes fastest.
Arguments:
- features: bfloat16 [4, 16, 8, 8, 512], P(('groups', 'dp'), 'space'), parts along dimension 0, may hold values from -6 to 6
- cotangent: bfloat16 [4, 16, 8, 8, 512], P(('groups', 'dp'), 'space'), parts along dimension 0, may hold values from -6 to 6
- kernel: bfloat16 [3, 3, 3, 64, 64], replicated, may hold values from -0.15625 to 0.15625
- neighbours: int32 [4, 16, 6], P(('groups', 'dp'), 'space'), parts along dimension 0, may hold values from -1 to 15, as said below
Outputs:
- response: bfloat16 [4, 16, 8, 8, 512], P(('groups', 'dp'), 'space'), parts along dimension 0
- feature_grad: bfloat16 [4, 16, 8, 8, 512], P(('groups', 'dp'), 'space'), parts along dimension 0
- kernel_grad: float32 [6, 3, 3, 64, 64], P('groups'), parts along dimension 0
There are 2 independent parts, one for each index of `groups`. A program takes and returns all parts, laid end to end along the dimension named above; an argument that names none is the same for every part. Nothing has to cross between parts.
Inputs may be any that keep to these rules, and one draw needn't show every extreme that they name: `neighbours`: the active bricks lie on a lattice of 3 by 8 by 4 bricks. Tile t sits at position p = t + 2: it covers lattice row p // 4 of the first dimension, rows 2 * (p % 4) to 2 * (p % 4) + 1 of the second and all rows of the third; it holds exactly 2 active bricks, in slots 2 * t to 2 * t + 1, listed by second then third lattice coordinate. In each realization one third-dimension row z is drawn, and every tile holds the bricks at z in its first and in its last second-dimension row; its other bricks are drawn at random. Directions are first dimension down, up, second down, up, third down, up; the relation is symmetric (if brick u is the up neighbour of s, s is the down neighbour of u), and -1 marks a neighbour that is inactive or outside the lattice.
All inputs are finite; a program needn't handle non-finite values.
Results may differ from a plain program's by a relative error of at most 0.0045.
Values may be sent and summed in bfloat16 or wider, within the bound.
No kernel may reach another device: no remote copies, remote signals or barrier semaphores. Data moves between devices by JAX's collectives and lax.ppermute only.
A program may use at most 64 MiB of HBM per device.

v0:
```python
import math
import jax
import jax.numpy as jnp
from jax import lax
from jax.sharding import PartitionSpec as P

TILES_Y = 4


def shifted(x, axis, by):
    count = lax.axis_size(axis)
    pairs = [(i, i + by) for i in range(count) if 0 <= i + by < count]
    return lax.ppermute(x, axis, pairs)


def choose_rows(tables, shifts, column, source_device, flat_slot, present, position):
    stacked = jnp.concatenate(tables, axis=0)
    row_count = tables[0].shape[0]
    source_pick = jnp.zeros_like(flat_slot[:, column])
    for number, offset in enumerate(shifts):
        source_pick = jnp.where(source_device[:, column] == position + offset, number, source_pick)
    row_index = source_pick * row_count + flat_slot[:, column]
    picked = jnp.take(stacked, row_index, axis=0)
    present_rows = present[:, column].reshape((-1,) + (1,) * (picked.ndim - 1))
    return jnp.where(present_rows, picked, jnp.zeros_like(picked))


def make_banded(weights, channels):
    toeplitz = jnp.zeros((3, 3, 4, channels, 2, channels), jnp.bfloat16)
    for out_cell in range(2):
        for tap_z in range(3):
            toeplitz = toeplitz.at[:, :, out_cell + tap_z, :, out_cell, :].set(weights[:, :, tap_z])
    return toeplitz.reshape(3, 3, 4 * channels, 2 * channels)


def make_windows(extended, channels, pairs_z):
    return jnp.stack(
        [
            extended[..., 2 * channels * block_index : 2 * channels * block_index + 4 * channels]
            for block_index in range(pairs_z)
        ],
        axis=3,
    )


def correlate(windows, banded, rows_all, brick_edge, pairs_z, channels):
    result = jnp.zeros((rows_all, brick_edge, brick_edge, pairs_z, 2 * channels), jnp.float32)
    for row_offset in range(3):
        for col_offset in range(3):
            window_part = windows[
                :, row_offset : row_offset + brick_edge, col_offset : col_offset + brick_edge
            ]
            result = result + jnp.einsum(
                "nabjk,kc->nabjc",
                window_part,
                banded[row_offset, col_offset],
                preferred_element_type=jnp.float32,
            )
    return result


def body(features, cotangent, kernel, neighbours):
    realizations = features.shape[0]
    bricks = features.shape[1]
    brick_edge = features.shape[2]
    channels = kernel.shape[-1]
    rows_all = realizations * bricks
    tile_stride = TILES_Y
    pairs_z = brick_edge // 2
    position = lax.axis_index("space")
    neighbour_slots = neighbours.reshape(rows_all, 6)
    present = neighbour_slots >= 0
    safe_links = jnp.where(present, neighbour_slots, 0)
    source_device = safe_links // bricks
    base_rows = jnp.repeat(jnp.arange(realizations, dtype=jnp.int32) * bricks, bricks)[:, None]
    flat_slot = base_rows + safe_links % bricks

    def select(tables, shifts, column):
        return choose_rows(tables, shifts, column, source_device, flat_slot, present, position)

    volume = features.reshape(rows_all, brick_edge, brick_edge, brick_edge * channels)
    upper_face = volume[:, brick_edge - 1]
    lower_face = volume[:, 0]
    from_below = shifted(upper_face, "space", tile_stride)
    from_above = shifted(lower_face, "space", -tile_stride)
    below_part = select([upper_face, from_below], [0, -tile_stride], 0)
    above_part = select([lower_face, from_above], [0, tile_stride], 1)
    layered_x = jnp.concatenate([below_part[:, None], volume, above_part[:, None]], axis=1)
    upper_face = layered_x[:, :, brick_edge - 1]
    lower_face = layered_x[:, :, 0]
    from_below = shifted(upper_face, "space", 1)
    from_above = shifted(lower_face, "space", -1)
    below_part = select([upper_face, from_below], [0, -1], 2)
    above_part = select([lower_face, from_above], [0, 1], 3)
    layered_y = jnp.concatenate([below_part[:, :, None], layered_x, above_part[:, :, None]], axis=2)
    upper_face = layered_y[..., (brick_edge - 1) * channels :]
    lower_face = layered_y[..., :channels]
    extended = jnp.concatenate(
        [select([upper_face], [0], 4), layered_y, select([lower_face], [0], 5)], axis=-1
    )
    banded = make_banded(kernel, channels)
    windows = make_windows(extended, channels, pairs_z)
    result = correlate(windows, banded, rows_all, brick_edge, pairs_z, channels)
    response = result.reshape(features.shape).astype(jnp.bfloat16)
    cotangent_pairs = cotangent.reshape(rows_all, brick_edge, brick_edge, pairs_z, 2 * channels)
    band_terms = []
    for row_offset in range(3):
        for col_offset in range(3):
            window_part = windows[
                :, row_offset : row_offset + brick_edge, col_offset : col_offset + brick_edge
            ]
            band_terms.append(
                jnp.einsum(
                    "nabjk,nabjc->kc",
                    window_part,
                    cotangent_pairs,
                    preferred_element_type=jnp.float32,
                )
            )
    band_grad = jnp.stack(band_terms).reshape(3, 3, 4, channels, 2, channels)
    kernel_local = jnp.stack(
        [
            band_grad[:, :, tap_z, :, 0, :] + band_grad[:, :, tap_z + 1, :, 1, :]
            for tap_z in range(3)
        ],
        axis=2,
    )
    cells_all = rows_all * lax.axis_size("dp") * lax.axis_size("space") * brick_edge**3
    factor = 1.0 / math.sqrt(cells_all)
    kernel_grad = lax.psum(kernel_local, ("space", "dp")) * factor
    spread = jnp.zeros(
        (rows_all, brick_edge + 2, brick_edge + 2, pairs_z, 4 * channels), jnp.float32
    )
    for row_offset in range(3):
        for col_offset in range(3):
            contribution = jnp.einsum(
                "nabjc,kc->nabjk",
                cotangent_pairs,
                banded[row_offset, col_offset],
                preferred_element_type=jnp.float32,
            )
            spread = spread.at[
                :, row_offset : row_offset + brick_edge, col_offset : col_offset + brick_edge
            ].add(contribution)
    widened = jnp.zeros(
        (rows_all, brick_edge + 2, brick_edge + 2, (brick_edge + 2) * channels), jnp.float32
    )
    for block_index in range(pairs_z):
        widened = widened.at[
            ..., 2 * channels * block_index : 2 * channels * block_index + 4 * channels
        ].add(spread[..., block_index, :])
    lower_rim = widened[..., :channels]
    upper_rim = widened[..., (brick_edge + 1) * channels :]
    trimmed_z = widened[..., channels : (brick_edge + 1) * channels]
    trimmed_z = trimmed_z.at[..., (brick_edge - 1) * channels :].add(select([lower_rim], [0], 5))
    trimmed_z = trimmed_z.at[..., :channels].add(select([upper_rim], [0], 4))
    lower_rim = trimmed_z[:, :, 0]
    upper_rim = trimmed_z[:, :, brick_edge + 1]
    trimmed_y = trimmed_z[:, :, 1 : brick_edge + 1]
    from_below = shifted(upper_rim.astype(jnp.bfloat16), "space", 1).astype(upper_rim.dtype)
    from_above = shifted(lower_rim.astype(jnp.bfloat16), "space", -1).astype(lower_rim.dtype)
    trimmed_y = trimmed_y.at[:, :, brick_edge - 1].add(select([lower_rim, from_above], [0, 1], 3))
    trimmed_y = trimmed_y.at[:, :, 0].add(select([upper_rim, from_below], [0, -1], 2))
    lower_rim = trimmed_y[:, 0]
    upper_rim = trimmed_y[:, brick_edge + 1]
    trimmed_x = trimmed_y[:, 1 : brick_edge + 1]
    from_below = shifted(upper_rim.astype(jnp.bfloat16), "space", tile_stride).astype(
        upper_rim.dtype
    )
    from_above = shifted(lower_rim.astype(jnp.bfloat16), "space", -tile_stride).astype(
        lower_rim.dtype
    )
    trimmed_x = trimmed_x.at[:, brick_edge - 1].add(
        select([lower_rim, from_above], [0, tile_stride], 1)
    )
    trimmed_x = trimmed_x.at[:, 0].add(select([upper_rim, from_below], [0, -tile_stride], 0))
    feature_grad = trimmed_x.reshape(features.shape).astype(jnp.bfloat16)
    return (response, feature_grad, kernel_grad)


def solution(mesh):
    in_specs = (
        P(("groups", "dp"), "space", None, None, None),
        P(("groups", "dp"), "space", None, None, None),
        P(),
        P(("groups", "dp"), "space", None),
    )
    out_specs = (
        P(("groups", "dp"), "space", None, None, None),
        P(("groups", "dp"), "space", None, None, None),
        P("groups", None, None, None, None),
    )
    return jax.shard_map(body, mesh=mesh, in_specs=in_specs, out_specs=out_specs, check_vma=False)
```

profile of v0, /device:TPU:0, one launch (start us, length us, event | category | flops | bytes accessed | tf_op | source)
XLA Modules:
  0.0 196.4 jit_solution(7922815339144183871)
XLA Ops:
  8.0 5.9 %collective-permute-start = (bf16[2,8,512]{2,1,0:T(8,128)(2,1)S(1)}, bf16[2,8,512]{2,1,0:T(8,128)(2,1)S(1)}, u32[]{:S(2)}, u32[]{:S(2)}) collective-permute-start(bf16[2,8,512]{2,1,0:T(8,128)(2,1)S(1)} %get-tuple-element.377), channel_id=1, source_target_pairs={{0,8},{2,10},{4,12},{6,14},{1,9},{3,11},{5,13},{7,15},{16,24},{18,... | collective-permute-start | bytes 49160 | tf_op jit(solution)/shard_map/ppermute | solution.py:13
  14.0 1.3 collective-permute-start.1
  19.5 1.2 copy.377
  22.5 1.5 fusion.10
  24.0 2.8 %scatter-add.65 = f32[2,10,10,4,256]{4,2,1,0,3:T(8,128)S(1)} dynamic-update-slice(f32[2,10,10,4,256]{4,2,1,0,3:T(8,128)S(1)} %scatter-add.64, f32[2,8,8,4,256]{4,2,1,0,3:T(8,128)S(1)} %fusion.10, s32[]{:T(128)} %constant.794.clone.1, s32[]{:T(128)} %bitcast.54, s32[]{:T(128)} %bitcast.55, s32[]{:T(128)} %constant.794.clone.1, s32[]{:T(128)} %constant.794.clone.1) | dynamic-update-slice | bytes 1048580 | tf_op jit(solution)/shard_map/scatter-add | solution.py:144
  26.9 2.1 %fusion.9 = f32[2,8,8,4,256]{4,2,1,0,3:T(8,128)S(1)} fusion(f32[2,10,10,4,256]{4,2,1,0,3:T(8,128)S(1)} %scatter-add.65, s32[]{:T(128)} %bitcast.59, s32[]{:T(128)} %bitcast.60, pred[]{:T(512)} %and_reduce_fusion, bf16[3,3,256,128]{3,2,1,0:T(8,128)(2,1)S(1)} %reshape.1187, bf16[1,2,8,8,512]{4,3,2,1,0:T(8,128)(2,1)S(1)} %copy-done), kind=kOutput, calls=%fused_computation.28 | convolution fusion | flops 33816576 | bytes 1245193 | tf_op jit(solution)/shard_map/nabjc,kc->nabjk/dot_general | solution.py:136
  29.0 2.9 %scatter-add.66 = f32[2,10,10,4,256]{4,2,1,0,3:T(8,128)S(1)} dynamic-update-slice(f32[2,10,10,4,256]{4,2,1,0,3:T(8,128)S(1)} %scatter-add.65, f32[2,8,8,4,256]{4,2,1,0,3:T(8,128)S(1)} %fusion.9, s32[]{:T(128)} %constant.794.clone.1, s32[]{:T(128)} %bitcast.59, s32[]{:T(128)} %bitcast.60, s32[]{:T(128)} %constant.794.clone.1, s32[]{:T(128)} %constant.794.clone.1) | dynamic-update-slice | bytes 1048580 | tf_op jit(solution)/shard_map/scatter-add | solution.py:144
  32.4 1.5 scatter-add.70
  34.2 1.5 scatter-add.71
  36.3 1.5 scatter-add.75
  38.0 1.5 scatter-add.76
  41.7 3.1 %scatter-add.85 = f32[2,10,10,512]{3,2,1,0:T(8,128)S(1)} dynamic-update-slice(f32[2,10,10,512]{3,2,1,0:T(8,128)S(1)} %slice.1260, f32[2,10,10,64]{3,2,1,0:T(8,128)S(1)} %get-tuple-element.368, s32[]{:T(128)} %constant.794.clone.1, s32[]{:T(128)} %constant.794.clone.1, s32[]{:T(128)} %constant.794.clone.1, s32[]{:T(128)} %constant.811.clone.1) | dynamic-update-slice | bytes 102404 | tf_op jit(solution)/shard_map/scatter-add | solution.py:155
  45.6 1.3 collective-permute-start.4
  46.9 4.5 %collective-permute-start.5 = (bf16[2,10,512]{2,0,1:T(2,128)(2,1)S(1)}, bf16[2,10,512]{2,0,1:T(2,128)(2,1)S(1)}, u32[]{:S(2)}, u32[]{:S(2)}) collective-permute-start(bf16[2,10,512]{2,0,1:T(2,128)(2,1)S(1)} %bitcast.421), channel_id=1, source_target_pairs={{0,2},{2,4},{4,6},{6,8},{8,10},{10,12},{12,14},{1,3},{3,5},{5,7},{... | collective-permute-start | bytes 61448 | tf_op jit(solution)/shard_map/ppermute | solution.py:13
  53.2 1.3 collective-permute-start.3
  54.5 4.9 %collective-permute-start.2 = (bf16[2,10,512]{2,1,0:T(8,128)(2,1)S(1)}, bf16[2,10,512]{2,1,0:T(8,128)(2,1)S(1)}, u32[]{:S(2)}, u32[]{:S(2)}) collective-permute-start(bf16[2,10,512]{2,1,0:T(8,128)(2,1)S(1)} %copy.364), channel_id=1, source_target_pairs={{0,2},{2,4},{4,6},{6,8},{8,10},{10,12},{12,14},{1,3},{3,5},{5,7},{... | collective-permute-start | bytes 61448 | tf_op jit(solution)/shard_map/ppermute | solution.py:13
  61.4 5.4 %collective-permute-start.7 = (bf16[2,8,512]{2,1,0:T(8,128)(2,1)S(1)}, bf16[2,8,512]{2,1,0:T(8,128)(2,1)S(1)}, u32[]{:S(2)}, u32[]{:S(2)}) collective-permute-start(bf16[2,8,512]{2,1,0:T(8,128)(2,1)S(1)} %get-tuple-element.365), channel_id=1, source_target_pairs={{0,8},{2,10},{4,12},{6,14},{1,9},{3,11},{5,13},{7,15},{16,24},{18,... | collective-permute-start | bytes 49160 | tf_op jit(solution)/shard_map/ppermute | solution.py:13
  66.9 1.5 collective-permute-start.6
  72.3 1.4 fusion.129
  78.4 0.9 fusion.20
  79.4 0.9 fusion.19
  80.3 0.9 fusion.18
  81.3 0.9 fusion.17
  83.2 0.9 fusion.15
  84.1 0.9 fusion.14
  85.0 0.9 fusion.13
  85.9 2.7 %reshape.1202 = f32[3,3,4,64,2,64]{5,4,3,2,1,0:T(2,128)S(1)} reshape(f32[9,256,128]{2,1,0:T(8,128)} %fusion.13) | data formatting | bytes 2359296 | tf_op jit(solution)/shard_map/reshape | solution.py:120
  88.6 1.9 fusion.128
  90.7 1.0 pad_maximum_fusion
  91.7 1.7 fusion.12
  93.4 94.0 %all-reduce.5.cloned.1.call-done = f32[3,3,3,64,64]{4,3,2,1,0:T(8,128)} async-done(((f32[3,3,3,64,64]{4,3,2,1,0:T(8,128)}), f32[3,3,3,64,64]{4,3,2,1,0:T(8,128)}) %all-reduce.5.cloned.1.call-update) | async-done | bytes 442384 | tf_op jit(solution)/shard_map/psum | solution.py:130
  187.4 2.2 %broadcast_multiply_fusion = f32[3,3,3,64,64]{4,3,2,1,0:T(8,128)} fusion(f32[3,3,3,64,64]{4,3,2,1,0:T(8,128)} %all-reduce.5.cloned.1.call-done), kind=kLoop, calls=%fused_computation.62 | loop fusion | flops 110592 | bytes 884736 | tf_op jit(solution)/shard_map/mul | solution.py:130
  (162 shorter events, 24.0 us)
Async XLA Ops:
  7.2 14.9 %copy-start = (bf16[1,2,8,8,512]{4,3,2,1,0:T(8,128)(2,1)S(1)}, bf16[1,2,8,8,512]{4,3,2,1,0:T(8,128)(2,1)}, u32[]{:S(2)}) copy-start(bf16[1,2,8,8,512]{4,3,2,1,0:T(8,128)(2,1)} %param.67) | copy-start | bytes 393220
  7.2 12.2 %copy-start.2 = (bf16[3,3,3,64,64]{4,3,2,1,0:T(8,128)(2,1)S(1)}, bf16[3,3,3,64,64]{4,3,2,1,0:T(8,128)(2,1)}, u32[]{:S(2)}) copy-start(bf16[3,3,3,64,64]{4,3,2,1,0:T(8,128)(2,1)} %param.68) | copy-start | bytes 663556
  7.2 180.2 %all-reduce.5.cloned.1.call-start = ((), (), s32[]{:S(2)}) async-start(), calls=%async_computation | async-start | bytes 1769472 | tf_op jit(solution)/shard_map/psum | solution.py:130
  8.0 43.7 %collective-permute-start = (bf16[2,8,512]{2,1,0:T(8,128)(2,1)S(1)}, bf16[2,8,512]{2,1,0:T(8,128)(2,1)S(1)}, u32[]{:S(2)}, u32[]{:S(2)}) collective-permute-start(bf16[2,8,512]{2,1,0:T(8,128)(2,1)S(1)} %get-tuple-element.377), channel_id=1, source_target_pairs={{0,8},{2,10},{4,12},{6,14},{1,9},{3,11},{5,13},{7,15},{16,24},{18,... | collective-permute-start | bytes 49160 | tf_op jit(solution)/shard_map/ppermute | solution.py:13
  14.0 38.3 %collective-permute-start.1 = (bf16[2,8,512]{2,1,0:T(8,128)(2,1)S(1)}, bf16[2,8,512]{2,1,0:T(8,128)(2,1)S(1)}, u32[]{:S(2)}, u32[]{:S(2)}) collective-permute-start(bf16[2,8,512]{2,1,0:T(8,128)(2,1)S(1)} %get-tuple-element.378), channel_id=1, source_target_pairs={{8,0},{10,2},{12,4},{14,6},{9,1},{11,3},{13,5},{15,7},{24,16},{26,... | collective-permute-start | bytes 49160 | tf_op jit(solution)/shard_map/ppermute | solution.py:13
  20.7 0.7 copy-start.10
  21.4 53.8 %copy-start.1 = (bf16[3,3,256,128]{3,2,1,0:T(8,128)(2,1)}, bf16[3,3,256,128]{3,2,1,0:T(8,128)(2,1)S(1)}, u32[]{:S(2)}) copy-start(bf16[3,3,256,128]{3,2,1,0:T(8,128)(2,1)S(1)} %reshape.1187) | copy-start | bytes 1769476
  44.9 8.1 %copy-start.3 = (bf16[1,2,8,8,512]{4,3,2,1,0:T(8,128)(2,1)S(1)}, bf16[1,2,8,8,512]{4,3,2,1,0:T(8,128)(2,1)}, u32[]{:S(2)}) copy-start(bf16[1,2,8,8,512]{4,3,2,1,0:T(8,128)(2,1)} %param.66) | copy-start | bytes 393220
  45.6 13.9 %collective-permute-start.4 = (bf16[2,10,512]{2,0,1:T(2,128)(2,1)S(1)}, bf16[2,10,512]{2,0,1:T(2,128)(2,1)S(1)}, u32[]{:S(2)}, u32[]{:S(2)}) collective-permute-start(bf16[2,10,512]{2,0,1:T(2,128)(2,1)S(1)} %bitcast.420), channel_id=1, source_target_pairs={{2,0},{4,2},{6,4},{8,6},{10,8},{12,10},{14,12},{3,1},{5,3},{7,5},{... | collective-permute-start | bytes 61448 | tf_op jit(solution)/shard_map/ppermute | solution.py:13
  46.9 12.5 %collective-permute-start.5 = (bf16[2,10,512]{2,0,1:T(2,128)(2,1)S(1)}, bf16[2,10,512]{2,0,1:T(2,128)(2,1)S(1)}, u32[]{:S(2)}, u32[]{:S(2)}) collective-permute-start(bf16[2,10,512]{2,0,1:T(2,128)(2,1)S(1)} %bitcast.421), channel_id=1, source_target_pairs={{0,2},{2,4},{4,6},{6,8},{8,10},{10,12},{12,14},{1,3},{3,5},{5,7},{... | collective-permute-start | bytes 61448 | tf_op jit(solution)/shard_map/ppermute | solution.py:13
  53.2 15.2 %collective-permute-start.3 = (bf16[2,10,512]{2,1,0:T(8,128)(2,1)S(1)}, bf16[2,10,512]{2,1,0:T(8,128)(2,1)S(1)}, u32[]{:S(2)}, u32[]{:S(2)}) collective-permute-start(bf16[2,10,512]{2,1,0:T(8,128)(2,1)S(1)} %copy.368), channel_id=1, source_target_pairs={{2,0},{4,2},{6,4},{8,6},{10,8},{12,10},{14,12},{3,1},{5,3},{7,5},{... | collective-permute-start | bytes 61448 | tf_op jit(solution)/shard_map/ppermute | solution.py:13
  54.5 14.6 %collective-permute-start.2 = (bf16[2,10,512]{2,1,0:T(8,128)(2,1)S(1)}, bf16[2,10,512]{2,1,0:T(8,128)(2,1)S(1)}, u32[]{:S(2)}, u32[]{:S(2)}) collective-permute-start(bf16[2,10,512]{2,1,0:T(8,128)(2,1)S(1)} %copy.364), channel_id=1, source_target_pairs={{0,2},{2,4},{4,6},{6,8},{8,10},{10,12},{12,14},{1,3},{3,5},{5,7},{... | collective-permute-start | bytes 61448 | tf_op jit(solution)/shard_map/ppermute | solution.py:13
  61.4 14.0 %collective-permute-start.7 = (bf16[2,8,512]{2,1,0:T(8,128)(2,1)S(1)}, bf16[2,8,512]{2,1,0:T(8,128)(2,1)S(1)}, u32[]{:S(2)}, u32[]{:S(2)}) collective-permute-start(bf16[2,8,512]{2,1,0:T(8,128)(2,1)S(1)} %get-tuple-element.365), channel_id=1, source_target_pairs={{0,8},{2,10},{4,12},{6,14},{1,9},{3,11},{5,13},{7,15},{16,24},{18,... | collective-permute-start | bytes 49160 | tf_op jit(solution)/shard_map/ppermute | solution.py:13
  66.9 9.1 %collective-permute-start.6 = (bf16[2,8,512]{2,1,0:T(8,128)(2,1)S(1)}, bf16[2,8,512]{2,1,0:T(8,128)(2,1)S(1)}, u32[]{:S(2)}, u32[]{:S(2)}) collective-permute-start(bf16[2,8,512]{2,1,0:T(8,128)(2,1)S(1)} %get-tuple-element.366), channel_id=1, source_target_pairs={{8,0},{10,2},{12,4},{14,6},{9,1},{11,3},{13,5},{15,7},{24,16},{26,... | collective-permute-start | bytes 49160 | tf_op jit(solution)/shard_map/ppermute | solution.py:13
  75.4 2.1 %copy-start.9 = (bf16[2,8,8,4,256]{4,2,3,1,0:T(8,128)(2,1)S(1)}, bf16[2,8,8,4,256]{4,2,3,1,0:T(8,128)(2,1)}, u32[]{:S(2)}) copy-start(bf16[2,8,8,4,256]{4,2,3,1,0:T(8,128)(2,1)} %get-tuple-element.360) | copy-start | bytes 786436
  77.5 1.0 copy-start.8
  78.4 0.9 copy-start.7
  79.4 0.9 copy-start.6
  80.3 0.9 copy-start.5
  81.3 0.9 copy-start.4
Sparse Core Ops, SparseCore 0:
  91.8 95.5 all-reduce.4
where the time goes:
time: 197 us; the launch traced here: 196 us
  waiting for transfers between devices  94 us (48%)
  local copies, waits for them, and re-layouts  35.9 us (18%)
  starting transfers between devices  26.2 us (13%)
  matrix products  17.3 us (9%)
  between operations  15.1 us (8%)
  other arithmetic  7.91 us (4%)
    psum x1, waiting for transfers between devices, body(): kernel_grad = lax.psum(kernel_local, ('space', 'dp')) * factor  94 us
    ppermute x8, starting transfers between devices, shifted(): return lax.ppermute(x, axis, pairs)  26.2 us
    scatter-add x7, local copies, waits for them, and re-layouts, body(): spread = spread.at[:, row_offset:row_offset + brick_edge, col_offset:col_...  12 us
    dot_general x9, matrix products, body(): jnp.einsum('nabjk,nabjc->kc', window_part, cotangent_pairs, preferred_ele...  8.32 us
    gather x12, local copies, waits for them, and re-layouts, choose_rows(): picked = jnp.take(stacked, row_index, axis=0)  6.66 us
    dot_general x9, matrix products, body(): jnp.einsum('nabjc,kc->nabjk', cotangent_pairs, banded[row_offset, col_off...  5.35 us
  transfers between devices with their start and end apart: 9, of which 1 were waited for; matrix products, arithmetic and copies ran while one was open for 22% of the time, Pallas kernels for 0%

commit v1 on v0

--- a/solution.py
+++ b/solution.py
@@ -127,7 +127,7 @@
     )
     cells_all = rows_all * lax.axis_size("dp") * lax.axis_size("space") * brick_edge**3
     factor = 1.0 / math.sqrt(cells_all)
-    kernel_grad = lax.psum(kernel_local, ("space", "dp")) * factor
+    kernel_grad = jnp.sum(lax.all_gather(kernel_local, ("space", "dp")), axis=0) * factor
     spread = jnp.zeros(
         (rows_all, brick_edge + 2, brick_edge + 2, pairs_z, 4 * channels), jnp.float32
     )

time: 197 us -> 175 us (0.89)
  waiting for transfers between devices: 94 us -> 70.7 us
  other arithmetic: 7.91 us -> 15.2 us
  local copies, waits for them, and re-layouts: 35.9 us -> 32.8 us
    psum x1 -> x0, waiting for transfers between devices: 94 us -> none  [body(): kernel_grad = lax.psum(kernel_local, ('space', 'dp')) * factor]
    all_gather x0 -> x1, waiting for transfers between devices: none -> 57.9 us  [body(): lax.all_gather(kernel_local, ('space', 'dp'))]
    ppermute x8, waiting for transfers between devices: 0.02 us -> 12.7 us  [shifted(): return lax.ppermute(x, axis, pairs)]
    reduce_sum x0 -> x1, other arithmetic: none -> 6.89 us  [body(): jnp.sum(lax.all_gather(kernel_local, ('space', 'dp')), axis=0) * factor]
    mul x1, other arithmetic: 2.17 us -> 0.06 us  [body(): jnp.sum(lax.all_gather(kernel_local, ('space', 'dp')), axis=0) * factor]
  transfers between devices with their start and end apart: 9 -> 9, of which waited for: 1 -> 5; matrix products, arithmetic and copies ran while one was open for 22% -> 21% of each run, Pallas kernels for 0% -> 0%
where the time goes in v1:
time: 175 us
  waiting for transfers between devices  70.7 us (40%)
  local copies, waits for them, and re-layouts  32.8 us (19%)
  starting transfers between devices  24.4 us (14%)
  matrix products  16.6 us (9%)
  other arithmetic  15.2 us (9%)
  between operations  15 us (9%)
    all_gather x1, waiting for transfers between devices, body(): lax.all_gather(kernel_local, ('space', 'dp'))  57.9 us
    ppermute x8, starting transfers between devices, shifted(): return lax.ppermute(x, axis, pairs)  24.4 us
    ppermute x8, waiting for transfers between devices, shifted(): return lax.ppermute(x, axis, pairs)  12.7 us
    scatter-add x7, local copies, waits for them, and re-layouts, body(): spread = spread.at[:, row_offset:row_offset + brick_edge, col_offset:col_...  12 us
    dot_general x9, matrix products, body(): jnp.einsum('nabjk,nabjc->kc', window_part, cotangent_pairs, preferred_ele...  8.37 us
    reduce_sum x1, other arithmetic, body(): jnp.sum(lax.all_gather(kernel_local, ('space', 'dp')), axis=0) * factor  6.89 us
    gather x12, local copies, waits for them, and re-layouts, choose_rows(): picked = jnp.take(stacked, row_index, axis=0)  6.66 us
    dot_general x9, matrix products, body(): jnp.einsum('nabjc,kc->nabjk', cotangent_pairs, banded[row_offset, col_off...  5.39 us
  transfers between devices with their start and end apart: 9, of which 5 were waited for; matrix products, arithmetic and copies ran while one was open for 21% of the time, Pallas kernels for 0%

profile of v1, /device:TPU:0, one launch (start us, length us, event | category | flops | bytes accessed | tf_op | source)
XLA Modules:
  0.0 174.7 jit_solution(5723885706221244742)
XLA Ops:
  8.0 5.9 %collective-permute-start = (bf16[2,8,512]{2,1,0:T(8,128)(2,1)S(1)}, bf16[2,8,512]{2,1,0:T(8,128)(2,1)S(1)}, u32[]{:S(2)}, u32[]{:S(2)}) collective-permute-start(bf16[2,8,512]{2,1,0:T(8,128)(2,1)S(1)} %get-tuple-element.379), channel_id=1, source_target_pairs={{0,8},{2,10},{4,12},{6,14},{1,9},{3,11},{5,13},{7,15},{16,24},{18,... | collective-permute-start | bytes 49160 | tf_op jit(solution)/shard_map/ppermute | solution.py:13
  14.0 1.3 collective-permute-start.1
  17.9 2.6 %collective-permute-done.1 = bf16[2,8,512]{2,1,0:T(8,128)(2,1)S(1)} collective-permute-done((bf16[2,8,512]{2,1,0:T(8,128)(2,1)S(1)}, bf16[2,8,512]{2,1,0:T(8,128)(2,1)S(1)}, u32[]{:S(2)}, u32[]{:S(2)}) %collective-permute-start.1) | collective-permute-done | bytes 16416 | tf_op jit(solution)/shard_map/ppermute | solution.py:13
  21.1 1.1 pad_maximum_fusion.21
  22.2 1.3 collective-permute-start.3
  23.6 4.5 %collective-permute-start.2 = (bf16[2,10,512]{2,1,0:T(8,128)(2,1)S(1)}, bf16[2,10,512]{2,1,0:T(8,128)(2,1)S(1)}, u32[]{:S(2)}, u32[]{:S(2)}) collective-permute-start(bf16[2,10,512]{2,1,0:T(8,128)(2,1)S(1)} %copy.415), channel_id=1, source_target_pairs={{0,2},{2,4},{4,6},{6,8},{8,10},{10,12},{12,14},{1,3},{3,5},{5,7},{... | collective-permute-start | bytes 61448 | tf_op jit(solution)/shard_map/ppermute | solution.py:13
  34.0 0.9 fusion.20
  35.0 0.9 fusion.19
  35.9 0.9 fusion.18
  39.6 0.9 fusion.14
  41.5 2.7 %reshape.1202 = f32[3,3,4,64,2,64]{5,4,3,2,1,0:T(2,128)S(1)} reshape(f32[9,256,128]{2,1,0:T(8,128)} %fusion.13) | data formatting | bytes 2359296 | tf_op jit(solution)/shard_map/reshape | solution.py:120
  44.2 1.6 fusion.128
  45.8 1.0 pad_maximum_fusion
  47.3 1.2 copy.428
  50.1 1.5 fusion.10
  51.6 2.8 %scatter-add.65 = f32[2,10,10,4,256]{4,2,1,0,3:T(8,128)S(1)} dynamic-update-slice(f32[2,10,10,4,256]{4,2,1,0,3:T(8,128)S(1)} %scatter-add.64, f32[2,8,8,4,256]{4,2,1,0,3:T(8,128)S(1)} %fusion.10, s32[]{:T(128)} %constant.795.clone.1, s32[]{:T(128)} %bitcast.54, s32[]{:T(128)} %bitcast.55, s32[]{:T(128)} %constant.795.clone.1, s32[]{:T(128)} %constant.795.clone.1) | dynamic-update-slice | bytes 1048580 | tf_op jit(solution)/shard_map/scatter-add | solution.py:144
  55.8 2.2 %fusion.9 = f32[2,8,8,4,256]{4,2,1,0,3:T(8,128)S(1)} fusion(f32[2,10,10,4,256]{4,2,1,0,3:T(8,128)S(1)} %scatter-add.65, s32[]{:T(128)} %bitcast.59, s32[]{:T(128)} %bitcast.60, pred[]{:T(512)} %and_reduce_fusion, bf16[3,3,256,128]{3,2,1,0:T(8,128)(2,1)S(1)} %reshape.1187, bf16[1,2,8,8,512]{4,3,2,1,0:T(8,128)(2,1)S(1)} %copy-done), kind=kOutput, calls=%fused_computation.28 | convolution fusion | flops 33816576 | bytes 1245193 | tf_op jit(solution)/shard_map/nabjc,kc->nabjk/dot_general | solution.py:136
  58.0 2.8 %scatter-add.66 = f32[2,10,10,4,256]{4,2,1,0,3:T(8,128)S(1)} dynamic-update-slice(f32[2,10,10,4,256]{4,2,1,0,3:T(8,128)S(1)} %scatter-add.65, f32[2,8,8,4,256]{4,2,1,0,3:T(8,128)S(1)} %fusion.9, s32[]{:T(128)} %constant.795.clone.1, s32[]{:T(128)} %bitcast.59, s32[]{:T(128)} %bitcast.60, s32[]{:T(128)} %constant.795.clone.1, s32[]{:T(128)} %constant.795.clone.1) | dynamic-update-slice | bytes 1048580 | tf_op jit(solution)/shard_map/scatter-add | solution.py:144
  61.3 1.5 scatter-add.70
  63.1 1.5 scatter-add.71
  65.2 1.5 scatter-add.75
  67.0 1.5 scatter-add.76
  70.4 3.1 %scatter-add.85 = f32[2,10,10,512]{3,2,1,0:T(8,128)S(1)} dynamic-update-slice(f32[2,10,10,512]{3,2,1,0:T(8,128)S(1)} %slice.1260, f32[2,10,10,64]{3,2,1,0:T(8,128)S(1)} %get-tuple-element.370, s32[]{:T(128)} %constant.795.clone.1, s32[]{:T(128)} %constant.795.clone.1, s32[]{:T(128)} %constant.795.clone.1, s32[]{:T(128)} %constant.812.clone.1) | dynamic-update-slice | bytes 102404 | tf_op jit(solution)/shard_map/scatter-add | solution.py:155
  74.2 4.3 %collective-permute-start.5 = (bf16[2,10,512]{2,0,1:T(2,128)(2,1)S(1)}, bf16[2,10,512]{2,0,1:T(2,128)(2,1)S(1)}, u32[]{:S(2)}, u32[]{:S(2)}) collective-permute-start(bf16[2,10,512]{2,0,1:T(2,128)(2,1)S(1)} %bitcast.419), channel_id=1, source_target_pairs={{0,2},{2,4},{4,6},{6,8},{8,10},{10,12},{12,14},{1,3},{3,5},{5,7},{... | collective-permute-start | bytes 61448 | tf_op jit(solution)/shard_map/ppermute | solution.py:13
  78.6 1.3 collective-permute-start.4
  80.7 4.8 %collective-permute-done.4 = bf16[2,10,512]{2,0,1:T(2,128)(2,1)S(1)} collective-permute-done((bf16[2,10,512]{2,0,1:T(2,128)(2,1)S(1)}, bf16[2,10,512]{2,0,1:T(2,128)(2,1)S(1)}, u32[]{:S(2)}, u32[]{:S(2)}) %collective-permute-start.4) | collective-permute-done | bytes 20512 | tf_op jit(solution)/shard_map/ppermute | solution.py:13
  86.7 4.2 %collective-permute-start.7 = (bf16[2,8,512]{2,1,0:T(8,128)(2,1)S(1)}, bf16[2,8,512]{2,1,0:T(8,128)(2,1)S(1)}, u32[]{:S(2)}, u32[]{:S(2)}) collective-permute-start(bf16[2,8,512]{2,1,0:T(8,128)(2,1)S(1)} %get-tuple-element.367), channel_id=1, source_target_pairs={{0,8},{2,10},{4,12},{6,14},{1,9},{3,11},{5,13},{7,15},{16,24},{18,... | collective-permute-start | bytes 49160 | tf_op jit(solution)/shard_map/ppermute | solution.py:13
  91.0 1.5 collective-permute-start.6
  93.1 4.5 %collective-permute-done.6 = bf16[2,8,512]{2,1,0:T(8,128)(2,1)S(1)} collective-permute-done((bf16[2,8,512]{2,1,0:T(8,128)(2,1)S(1)}, bf16[2,8,512]{2,1,0:T(8,128)(2,1)S(1)}, u32[]{:S(2)}, u32[]{:S(2)}) %collective-permute-start.6) | collective-permute-done | bytes 16416 | tf_op jit(solution)/shard_map/ppermute | solution.py:13
  101.9 57.9 %all-gather.3.cloned.1.call-done = f32[48,3,3,64,64]{4,3,1,0,2:T(8,128)} async-done(((f32[3,3,3,64,64]{4,3,1,0,2:T(8,128)}), f32[48,3,3,64,64]{4,3,1,0,2:T(8,128)}) %all-gather.3.cloned.1.call-update) | async-done | bytes 7077904 | tf_op jit(solution)/shard_map/all_gather | solution.py:130
  159.9 6.9 %reduce_sum.9 = f32[3,3,3,64,64]{4,3,1,0,2:T(8,128)S(1)} reduce(f32[16,3,3,3,64,64]{5,4,2,1,0,3:T(8,128)} %bitcast.403, f32[]{:T(128)} %constant.805.clone.1), dimensions={0}, to_apply=%region_1.8 | reduce | flops 1658880 | bytes 7520260 | tf_op jit(solution)/shard_map/reduce_sum | solution.py:130
  166.8 1.0 copy.471
  (149 shorter events, 27.8 us)
Async XLA Ops:
  7.2 25.9 %copy-start = (bf16[1,2,8,8,512]{4,3,2,1,0:T(8,128)(2,1)S(1)}, bf16[1,2,8,8,512]{4,3,2,1,0:T(8,128)(2,1)}, u32[]{:S(2)}) copy-start(bf16[1,2,8,8,512]{4,3,2,1,0:T(8,128)(2,1)} %param.67) | copy-start | bytes 393220
  7.2 23.2 %copy-start.2 = (bf16[1,2,8,8,512]{4,3,2,1,0:T(8,128)(2,1)S(1)}, bf16[1,2,8,8,512]{4,3,2,1,0:T(8,128)(2,1)}, u32[]{:S(2)}) copy-start(bf16[1,2,8,8,512]{4,3,2,1,0:T(8,128)(2,1)} %param.66) | copy-start | bytes 393220
  7.2 152.7 %all-gather.3.cloned.1.call-start = ((), (), s32[]{:S(2)}) async-start(), calls=%async_computation | async-start | bytes 15040512 | tf_op jit(solution)/shard_map/all_gather | solution.py:130
  8.0 9.3 %collective-permute-start = (bf16[2,8,512]{2,1,0:T(8,128)(2,1)S(1)}, bf16[2,8,512]{2,1,0:T(8,128)(2,1)S(1)}, u32[]{:S(2)}, u32[]{:S(2)}) collective-permute-start(bf16[2,8,512]{2,1,0:T(8,128)(2,1)S(1)} %get-tuple-element.379), channel_id=1, source_target_pairs={{0,8},{2,10},{4,12},{6,14},{1,9},{3,11},{5,13},{7,15},{16,24},{18,... | collective-permute-start | bytes 49160 | tf_op jit(solution)/shard_map/ppermute | solution.py:13
  14.0 6.5 %collective-permute-start.1 = (bf16[2,8,512]{2,1,0:T(8,128)(2,1)S(1)}, bf16[2,8,512]{2,1,0:T(8,128)(2,1)S(1)}, u32[]{:S(2)}, u32[]{:S(2)}) collective-permute-start(bf16[2,8,512]{2,1,0:T(8,128)(2,1)S(1)} %get-tuple-element.380), channel_id=1, source_target_pairs={{8,0},{10,2},{12,4},{14,6},{9,1},{11,3},{13,5},{15,7},{24,16},{26,... | collective-permute-start | bytes 49160 | tf_op jit(solution)/shard_map/ppermute | solution.py:13
  22.2 5.9 %collective-permute-start.3 = (bf16[2,10,512]{2,1,0:T(8,128)(2,1)S(1)}, bf16[2,10,512]{2,1,0:T(8,128)(2,1)S(1)}, u32[]{:S(2)}, u32[]{:S(2)}) collective-permute-start(bf16[2,10,512]{2,1,0:T(8,128)(2,1)S(1)} %copy.419), channel_id=1, source_target_pairs={{2,0},{4,2},{6,4},{8,6},{10,8},{12,10},{14,12},{3,1},{5,3},{7,5},{... | collective-permute-start | bytes 61448 | tf_op jit(solution)/shard_map/ppermute | solution.py:13
  23.6 6.1 %collective-permute-start.2 = (bf16[2,10,512]{2,1,0:T(8,128)(2,1)S(1)}, bf16[2,10,512]{2,1,0:T(8,128)(2,1)S(1)}, u32[]{:S(2)}, u32[]{:S(2)}) collective-permute-start(bf16[2,10,512]{2,1,0:T(8,128)(2,1)S(1)} %copy.415), channel_id=1, source_target_pairs={{0,2},{2,4},{4,6},{6,8},{8,10},{10,12},{12,14},{1,3},{3,5},{5,7},{... | collective-permute-start | bytes 61448 | tf_op jit(solution)/shard_map/ppermute | solution.py:13
  45.8 1.1 copy-start.1
  49.5 5.6 %copy-start.3 = (s32[5]{0:T(128)S(1)}, s32[5]{0:T(128)}, u32[]{:S(2)}) copy-start(s32[5]{0:T(128)} %constant.807.clone.1) | copy-start | bytes 64
  74.2 5.8 %collective-permute-start.5 = (bf16[2,10,512]{2,0,1:T(2,128)(2,1)S(1)}, bf16[2,10,512]{2,0,1:T(2,128)(2,1)S(1)}, u32[]{:S(2)}, u32[]{:S(2)}) collective-permute-start(bf16[2,10,512]{2,0,1:T(2,128)(2,1)S(1)} %bitcast.419), channel_id=1, source_target_pairs={{0,2},{2,4},{4,6},{6,8},{8,10},{10,12},{12,14},{1,3},{3,5},{5,7},{... | collective-permute-start | bytes 61448 | tf_op jit(solution)/shard_map/ppermute | solution.py:13
  78.6 6.9 %collective-permute-start.4 = (bf16[2,10,512]{2,0,1:T(2,128)(2,1)S(1)}, bf16[2,10,512]{2,0,1:T(2,128)(2,1)S(1)}, u32[]{:S(2)}, u32[]{:S(2)}) collective-permute-start(bf16[2,10,512]{2,0,1:T(2,128)(2,1)S(1)} %bitcast.418), channel_id=1, source_target_pairs={{2,0},{4,2},{6,4},{8,6},{10,8},{12,10},{14,12},{3,1},{5,3},{7,5},{... | collective-permute-start | bytes 61448 | tf_op jit(solution)/shard_map/ppermute | solution.py:13
  86.7 5.8 %collective-permute-start.7 = (bf16[2,8,512]{2,1,0:T(8,128)(2,1)S(1)}, bf16[2,8,512]{2,1,0:T(8,128)(2,1)S(1)}, u32[]{:S(2)}, u32[]{:S(2)}) collective-permute-start(bf16[2,8,512]{2,1,0:T(8,128)(2,1)S(1)} %get-tuple-element.367), channel_id=1, source_target_pairs={{0,8},{2,10},{4,12},{6,14},{1,9},{3,11},{5,13},{7,15},{16,24},{18,... | collective-permute-start | bytes 49160 | tf_op jit(solution)/shard_map/ppermute | solution.py:13
  91.0 6.6 %collective-permute-start.6 = (bf16[2,8,512]{2,1,0:T(8,128)(2,1)S(1)}, bf16[2,8,512]{2,1,0:T(8,128)(2,1)S(1)}, u32[]{:S(2)}, u32[]{:S(2)}) collective-permute-start(bf16[2,8,512]{2,1,0:T(8,128)(2,1)S(1)} %get-tuple-element.368), channel_id=1, source_target_pairs={{8,0},{10,2},{12,4},{14,6},{9,1},{11,3},{13,5},{15,7},{24,16},{26,... | collective-permute-start | bytes 49160 | tf_op jit(solution)/shard_map/ppermute | solution.py:13
Sparse Core Ops, SparseCore 0:
  47.0 112.8 all-gather.2
